TPU v7x, 32 devices: a whole 2x2x4 slice. The times are simulated.
32 devices in a mesh: stick: 2 (over x), band: 16 (over z, y, core).
Axes of the slice: x: 2, y: 2, z: 4, core: 2. Of those that a mesh axis runs over, the one named last changes fastest.
Arguments:
- orbital_sticks: bfloat16 [32, 6144, 128], P('band', 'stick'), may hold values from -5 to 5
- stick_perm: int32 [4096], replicated, may hold values from 0 to 4095, each once
- stick_counts: int32 [2], replicated, may hold values from 1 to 3072, 4096 in all
- source_ids: int32 [1], replicated, may hold values from 0 to 31
Outputs:
- exchange: bfloat16 [32, 64, 64, 128], P(('band', 'stick'))
All inputs are finite; a program needn't handle non-finite values.
Results may differ from a plain program's by a relative error of at most 0.001.
Values may be sent and summed in bfloat16 or wider, within the bound.
A program may use at most 64 MiB of HBM per device.

v0:
```python
import math
import jax
import jax.numpy as jnp
from jax import lax
from jax.sharding import PartitionSpec as P

NX = 64
NY = 64
NZ = 128
screen_omega = 0.25


def broadcast(array, axis, root):
    mine = lax.axis_index(axis) == root
    return lax.psum(jnp.where(mine, array, jnp.zeros_like(array)), axis)


def slot_targets(stick_perm, stick_counts, capacity, slot_total):
    slots = jnp.arange(slot_total, dtype=jnp.int32)
    holder = slots // capacity
    within = slots % capacity
    offsets = jnp.cumsum(stick_counts) - stick_counts
    valid = within < stick_counts[holder]
    position = jnp.clip(offsets[holder] + within, 0, NX * NY - 1)
    return jnp.where(valid, stick_perm[position], NX * NY)


def place_sticks(blocks, targets):
    empty = jnp.zeros((blocks.shape[0], NX * NY + 1, NZ), blocks.dtype)
    filled = empty.at[:, targets].set(blocks)
    return filled[:, : NX * NY].reshape(blocks.shape[0], NX, NY, NZ)


def signed_freq(length):
    steps = jnp.arange(length, dtype=jnp.int32)
    signed = jnp.where(steps <= length // 2, steps, steps - length)
    return signed.astype(jnp.float32) / length


def screened(freq_x, freq_y, freq_z):
    square = (2.0 * math.pi) ** 2 * (
        freq_x[:, None, None] ** 2 + freq_y[None, :, None] ** 2 + freq_z[None, None, :] ** 2
    )
    safe = jnp.where(square > 0, square, 1.0)
    inner = 4.0 * math.pi * (1.0 - jnp.exp(-square / (4.0 * screen_omega**2))) / safe
    return jnp.where(square > 0, inner, math.pi / screen_omega**2)


def hartley_table(length):
    steps = jnp.arange(length, dtype=jnp.int32)
    product = steps[:, None] * steps[None, :] % length
    angle = product.astype(jnp.float32) * (2.0 * math.pi / length)
    return jnp.cos(angle) + jnp.sin(angle)


def hartley(field, table_x, table_y, table_z):
    highest = lax.Precision.HIGHEST
    section = jnp.einsum("bxyz,zc->bxyc", field, table_z, precision=highest)
    section = jnp.einsum("bxyc,yd->bxdc", section, table_y, precision=highest)
    return jnp.einsum("bxdc,xe->bedc", section, table_x, precision=highest)


def local(orbital_sticks, stick_perm, stick_counts, source_ids):
    stick_total = lax.axis_size("stick")
    rows, capacity, depth = orbital_sticks.shape
    targets = slot_targets(stick_perm, stick_counts, capacity, stick_total * capacity)
    regrouped = lax.all_to_all(orbital_sticks, "stick", split_axis=0, concat_axis=1, tiled=True)
    owned = place_sticks(regrouped, targets)
    table_x = hartley_table(NX)
    table_y = hartley_table(NY)
    table_z = hartley_table(NZ)
    kernel = screened(signed_freq(NX), signed_freq(NY), signed_freq(NZ))
    orbital_id = source_ids[0]
    group = orbital_id // rows
    local_row = orbital_id % rows
    piece = lax.dynamic_index_in_dim(orbital_sticks, local_row, 0, keepdims=False)
    piece = broadcast(piece, "band", group)
    blocks = lax.all_gather(piece, "stick", axis=0, tiled=True)
    source = place_sticks(blocks[None], targets)[0]
    source_value = source.astype(jnp.float32)[None]
    density = owned.astype(jnp.float32) * source_value
    spectrum = hartley(density, table_x, table_y, table_z) * kernel[None]
    potential = hartley(spectrum, table_x, table_y, table_z) / (NX * NY * NZ)
    total = source_value * potential
    return (-total).astype(jnp.bfloat16)


def solution(mesh):
    placed = (P("band", "stick", None), P(), P(), P())
    return jax.shard_map(
        local,
        mesh=mesh,
        in_specs=placed,
        out_specs=P(("band", "stick"), None, None, None),
        check_vma=False,
    )
```

profile of v0, /device:TPU:0, one launch (start us, length us, event | category | flops | bytes accessed | tf_op | source)
XLA Modules:
  0.0 207.3 jit_solution(2869489448109365349)
XLA Ops:
  6.5 0.0 copy-start
  6.5 0.0 copy-start.1
  6.5 0.0 copy-start.3
  6.5 4.4 %all-to-all-start = ((bf16[2,3072,128]{2,1,0:T(8,128)(2,1)}), bf16[2,3072,128]{2,1,0:T(8,128)(2,1)S(1)}, u32[]{:S(2)}, u32[]{:S(2)}) async-start(bf16[2,3072,128]{2,1,0:T(8,128)(2,1)} %param.4), calls=%async_computation | async-start | bytes 3145728 | tf_op jit(solution)/shard_map/all_to_all | solution.py:67
  10.9 0.0 all-reduce.2.cloned.1.call-start
  11.6 0.0 copy-done.1
  11.6 0.9 select_bitcast_fusion
  12.5 0.0 all-reduce.2.cloned.1.call-update
  12.6 0.0 all-gather.2.cloned.1.call-start
  12.6 0.0 copy-done.3
  12.6 0.2 reduce-window.9
  12.8 0.6 fusion.85
  13.4 1.3 compare_select_fusion.3
  14.8 0.7 fusion.84
  15.4 95.2 %all-reduce.2.cloned.1.call-done = bf16[3072,128]{1,0:T(8,128)(2,1)} async-done(((bf16[3072,128]{1,0:T(8,128)(2,1)}), bf16[3072,128]{1,0:T(8,128)(2,1)}) %all-reduce.2.cloned.1.call-update) | async-done | bytes 786448 | tf_op jit(solution)/shard_map/psum | solution.py:15
  110.6 0.0 all-gather.2.cloned.1.call-update
  110.6 0.0 copy-done
  110.6 34.3 %gather_fusion = s32[6144]{0:T(1024)S(1)} fusion(s32[4096]{0:T(1024)S(1)} %copy-done, s32[6144]{0:T(1024)S(1)} %broadcast_clamp_fusion), kind=kCustom, calls=%fused_computation | custom fusion | bytes 73728 | tf_op jit(solution)/shard_map/gather | solution.py:25
  144.9 0.1 broadcast_add_fusion
  145.0 1.5 compare_select_fusion.2
  146.5 0.0 all-to-all-done
  146.5 0.0 copy-start.2
  146.5 1.1 copy-done.2
  147.6 16.5 %scatter_custom_fusion.1 = bf16[4097,128]{1,0:T(8,128)(2,1)S(1)} fusion(s32[6144]{0:T(1024)S(1)} %bitcast.64, bf16[6144,128]{1,0:T(8,128)(2,1)} %bitcast.61, bf16[]{:T(256)} %constant.104.clone.1), kind=kCustom, calls=%fused_computation.29 | custom fusion | bytes 1049344 | tf_op jit(solution)/shard_map/scatter | solution.py:30
  164.1 0.1 slice.17
  164.2 0.0 all-gather.2.cloned.1.call-done
  164.2 16.7 %scatter_custom_fusion = bf16[4097,128]{1,0:T(8,128)(2,1)S(1)} fusion(s32[6144]{0:T(1024)S(1)} %bitcast.65, bf16[6144,128]{1,0:T(8,128)(2,1)} %all-gather.2.cloned.1.call-done, bf16[]{:T(256)} %constant.104.clone.1), kind=kCustom, calls=%fused_computation.31 | custom fusion | bytes 1049344 | tf_op jit(solution)/shard_map/scatter | solution.py:30
  180.9 0.1 slice.16
  181.0 0.2 convert.2
  181.2 2.1 %fusion.2 = f32[64,64,128]{2,1,0:T(8,128)S(1)} fusion(bf16[64,64,128]{2,1,0:T(8,128)(2,1)S(1)} %bitcast.60, bf16[64,64,128]{2,1,0:T(8,128)(2,1)S(1)} %bitcast.57), kind=kOutput, calls=%fused_computation.8 | convolution fusion | flops 807124992 | bytes 4194304 | tf_op jit(solution)/shard_map/bxyz,zc->bxyc/dot_general | solution.py:58
  183.3 2.1 %convolution_bitcast_fusion.1 = f32[64,64,128]{2,1,0:T(8,128)S(1)} fusion(f32[64,64,128]{2,1,0:T(8,128)S(1)} %fusion.2), kind=kOutput, calls=%fused_computation.18 | convolution fusion | flops 402714624 | bytes 4194304 | tf_op jit(solution)/shard_map/bxyc,yd->bxdc/dot_general | solution.py:59
  185.4 3.1 %fusion.3 = f32[64,64,128]{2,0,1:T(8,128)S(1)} fusion(f32[64,64,128]{2,1,0:T(8,128)S(1)} %convolution_bitcast_fusion.1), kind=kOutput, calls=%fused_computation.9 | convolution fusion | flops 402714624 | bytes 4194304 | tf_op jit(solution)/shard_map/bxdc,xe->bedc/dot_general | solution.py:60
  188.5 3.7 %fusion.9 = f32[64,64,128]{2,1,0:T(8,128)S(1)} fusion(f32[64,64,128]{2,0,1:T(8,128)S(1)} %fusion.3, f32[128]{0:T(128)S(1)} %fusion.53, f32[64,64]{1,0:T(8,128)S(1)} %broadcast_add_fusion), kind=kOutput, calls=%fused_computation.16 | convolution fusion | flops 811319296 | bytes 4211200 | tf_op jit(solution)/shard_map/bxyz,zc->bxyc/dot_general | solution.py:58
  192.2 2.3 %convolution_bitcast_fusion = f32[64,64,128]{2,1,0:T(8,128)S(1)} fusion(f32[64,64,128]{2,1,0:T(8,128)S(1)} %fusion.9), kind=kOutput, calls=%fused_computation.17 | convolution fusion | flops 402714624 | bytes 4194304 | tf_op jit(solution)/shard_map/bxyc,yd->bxdc/dot_general | solution.py:59
  194.6 4.3 %fusion.13 = bf16[1,64,64,128]{3,1,2,0:T(8,128)(2,1)S(1)} fusion(f32[64,64,128]{2,1,0:T(8,128)S(1)} %convolution_bitcast_fusion, f32[64,64,128]{2,1,0:T(8,128)S(1)} %convert.2), kind=kOutput, calls=%fused_computation.19 | convolution fusion | flops 404811776 | bytes 5242880 | tf_op jit(solution)/shard_map/bxdc,xe->bedc/dot_general | solution.py:60
  198.8 1.6 copy.9
  (4 shorter events, 0.0 us)
Async XLA Ops:
  6.5 104.1 %copy-start = (s32[4096]{0:T(1024)S(1)}, s32[4096]{0:T(1024)}, u32[]{:S(2)}) copy-start(s32[4096]{0:T(1024)} %param.5) | copy-start | bytes 49156
  6.5 5.1 %copy-start.1 = (bf16[2,3072,128]{2,1,0:T(8,128)(2,1)S(1)}, bf16[2,3072,128]{2,1,0:T(8,128)(2,1)}, u32[]{:S(2)}) copy-start(bf16[2,3072,128]{2,1,0:T(8,128)(2,1)} %param.4) | copy-start | bytes 4718596
  6.5 6.1 %copy-start.3 = (s32[2]{0:T(128)S(1)}, s32[2]{0:T(128)}, u32[]{:S(2)}) copy-start(s32[2]{0:T(128)} %param.6) | copy-start | bytes 28
  6.5 139.9 %all-to-all-start = ((bf16[2,3072,128]{2,1,0:T(8,128)(2,1)}), bf16[2,3072,128]{2,1,0:T(8,128)(2,1)S(1)}, u32[]{:S(2)}, u32[]{:S(2)}) async-start(bf16[2,3072,128]{2,1,0:T(8,128)(2,1)} %param.4), calls=%async_computation | async-start | bytes 3145728 | tf_op jit(solution)/shard_map/all_to_all | solution.py:67
  10.9 99.7 %all-reduce.2.cloned.1.call-start = ((), (), s32[]{:S(2)}) async-start(), calls=%async_computation.1 | async-start | bytes 1572864 | tf_op jit(solution)/shard_map/psum | solution.py:15
  12.6 151.7 %all-gather.2.cloned.1.call-start = ((), (), s32[]{:S(2)}) async-start(), calls=%async_computation.2 | async-start | bytes 2359296 | tf_op jit(solution)/shard_map/all_gather | solution.py:78
  146.5 1.2 copy-start.2
Sparse Core Ops, SparseCore 0:
  15.1 95.4 all-reduce.1
  112.1 26.2 all-gather.1
where the time goes:
time: 208 us; the launch traced here: 207 us
  waiting for transfers between devices  95.2 us (46%)
  local copies, waits for them, and re-layouts  71.7 us (34%)
  matrix products  17.5 us (8%)
  between operations  14.3 us (7%)
  starting transfers between devices  4.41 us (2%)
  other arithmetic  4.23 us (2%)
    psum x1, waiting for transfers between devices, broadcast(): return lax.psum(jnp.where(mine, array, jnp.zeros_like(array)), axis)  95.2 us
    gather x1, local copies, waits for them, and re-layouts, slot_targets(): return jnp.where(valid, stick_perm[position], NX * NY)  34.3 us
    scatter x2, local copies, waits for them, and re-layouts, place_sticks(): filled = empty.at[:, targets].set(blocks)  33.2 us
    dot_general x2, matrix products, hartley(): return jnp.einsum('bxdc,xe->bedc', section, table_x, precision=highest)  7.35 us
    dot_general x2, matrix products, hartley(): section = jnp.einsum('bxyz,zc->bxyc', field, table_z, precision=highest)  5.73 us
    dot_general x2, matrix products, hartley(): section = jnp.einsum('bxyc,yd->bxdc', section, table_y, precision=highest)  4.45 us
    all_to_all x1, starting transfers between devices, local(): lax.all_to_all(orbital_sticks, 'stick', split_axis=0, concat_axis=1, tile...  4.37 us
  transfers between devices with their start and end apart: 3, of which 1 were waited for; matrix products, arithmetic and copies ran while one was open for 27% of the time, Pallas kernels for 0%

commit v1 on v0

--- a/solution.py
+++ b/solution.py
@@ -12,7 +12,7 @@
 
 def broadcast(array, axis, root):
     mine = lax.axis_index(axis) == root
-    return lax.psum(jnp.where(mine, array, jnp.zeros_like(array)), axis)
+    return jnp.sum(lax.all_gather(jnp.where(mine, array, jnp.zeros_like(array)), axis), axis=0)
 
 
 def slot_targets(stick_perm, stick_counts, capacity, slot_total):

time: 208 us -> 218 us (1.048)
  other arithmetic: 4.23 us -> 12.8 us
    all_gather x0 -> x1, waiting for transfers between devices: none -> 96.4 us  [broadcast(): lax.all_gather(jnp.where(mine, array, jnp.zeros_like(array)), axis)]
    psum x1 -> x0, waiting for transfers between devices: 95.2 us -> none  [broadcast(): return lax.psum(jnp.where(mine, array, jnp.zeros_like(array)), axis)]
    reduce_sum x0 -> x1, other arithmetic: none -> 7.44 us  [broadcast(): jnp.sum(lax.all_gather(jnp.where(mine, array, jnp.zeros_like(array)), axi...]
  transfers between devices with their start and end apart: 3 -> 3, of which waited for: 1 -> 1; matrix products, arithmetic and copies ran while one was open for 27% -> 29% of each run, Pallas kernels for 0% -> 0%
where the time goes in v1:
time: 218 us
  waiting for transfers between devices  96.5 us (44%)
  local copies, waits for them, and re-layouts  71.6 us (33%)
  matrix products  18.6 us (9%)
  between operations  14.2 us (7%)
  other arithmetic  12.8 us (6%)
  starting transfers between devices  4.25 us (2%)
    all_gather x1, waiting for transfers between devices, broadcast(): lax.all_gather(jnp.where(mine, array, jnp.zeros_like(array)), axis)  96.4 us
    gather x1, local copies, waits for them, and re-layouts, slot_targets(): return jnp.where(valid, stick_perm[position], NX * NY)  34.3 us
    scatter x2, local copies, waits for them, and re-layouts, place_sticks(): filled = empty.at[:, targets].set(blocks)  33.2 us
    dot_general x2, matrix products, hartley(): return jnp.einsum('bxdc,xe->bedc', section, table_x, precision=highest)  8.48 us
    reduce_sum x1, other arithmetic, broadcast(): jnp.sum(lax.all_gather(jnp.where(mine, array, jnp.zeros_like(array)), axi...  7.44 us
    dot_general x2, matrix products, hartley(): section = jnp.einsum('bxyz,zc->bxyc', field, table_z, precision=highest)  5.68 us
    dot_general x2, matrix products, hartley(): section = jnp.einsum('bxyc,yd->bxdc', section, table_y, precision=highest)  4.49 us
  transfers between devices with their start and end apart: 3, of which 1 were waited for; matrix products, arithmetic and copies ran while one was open for 29% of the time, Pallas kernels for 0%

profile of v1, /device:TPU:0, one launch (start us, length us, event | category | flops | bytes accessed | tf_op | source)
XLA Modules:
  0.0 218.0 jit_solution(8346414011918448218)
XLA Ops:
  6.5 0.0 copy-start
  6.5 0.0 all-gather.3.cloned.1.call-start
  7.2 2.1 dynamic-slice_select_fusion
  9.3 0.0 copy-start.2
  9.3 0.0 all-gather.3.cloned.1.call-update
  9.3 4.2 %all-to-all-start = ((bf16[2,3072,128]{2,1,0:T(8,128)(2,1)}), bf16[2,3072,128]{2,1,0:T(8,128)(2,1)S(1)}, u32[]{:S(2)}, u32[]{:S(2)}) async-start(bf16[2,3072,128]{2,1,0:T(8,128)(2,1)} %param.4), calls=%async_computation | async-start | bytes 3145728 | tf_op jit(solution)/shard_map/all_to_all | solution.py:67
  13.6 0.0 all-gather.5.cloned.1.call-start
  13.6 0.0 copy-done.2
  13.6 0.2 reduce-window.9
  13.8 0.6 fusion.72
  14.4 0.6 fusion.73
  15.0 1.4 compare_select_fusion.3
  16.4 96.4 %all-gather.3.cloned.1.call-done = bf16[16,3072,128]{2,1,0:T(8,128)(2,1)} async-done(((bf16[1,3072,128]{2,1,0:T(8,128)(2,1)}), bf16[16,3072,128]{2,1,0:T(8,128)(2,1)}) %all-gather.3.cloned.1.call-update) | async-done | bytes 12582928 | tf_op jit(solution)/shard_map/all_gather | solution.py:15
  112.8 7.4 %reduce_sum.12 = bf16[3072,128]{1,0:T(8,128)(2,1)} reduce(bf16[16,3072,128]{2,1,0:T(8,128)(2,1)} %all-gather.3.cloned.1.call-done, bf16[]{:T(256)} %constant.106.clone.1), dimensions={0}, to_apply=%region_1.2 | reduce | flops 5898240 | bytes 13369346 | tf_op jit(solution)/shard_map/reduce_sum | solution.py:15
  120.2 0.0 all-gather.5.cloned.1.call-update
  120.3 0.0 copy-done
  120.3 34.3 %gather_fusion = s32[6144]{0:T(1024)S(1)} fusion(s32[4096]{0:T(1024)S(1)} %copy-done, s32[6144]{0:T(1024)S(1)} %broadcast_clamp_fusion), kind=kCustom, calls=%fused_computation | custom fusion | bytes 73728 | tf_op jit(solution)/shard_map/gather | solution.py:25
  154.6 0.1 broadcast_add_fusion
  154.7 1.4 compare_select_fusion.2
  156.1 0.0 all-to-all-done
  156.1 0.0 copy-start.1
  156.1 1.1 copy-done.1
  157.2 16.5 %scatter_custom_fusion.1 = bf16[4097,128]{1,0:T(8,128)(2,1)S(1)} fusion(s32[6144]{0:T(1024)S(1)} %bitcast.60, bf16[6144,128]{1,0:T(8,128)(2,1)} %bitcast.57, bf16[]{:T(256)} %constant.106.clone.1), kind=kCustom, calls=%fused_computation.22 | custom fusion | bytes 1049344 | tf_op jit(solution)/shard_map/scatter | solution.py:30
  173.7 0.1 slice.17
  173.8 0.0 all-gather.5.cloned.1.call-done
  173.8 16.7 %scatter_custom_fusion = bf16[4097,128]{1,0:T(8,128)(2,1)S(1)} fusion(s32[6144]{0:T(1024)S(1)} %bitcast.61, bf16[6144,128]{1,0:T(8,128)(2,1)} %all-gather.5.cloned.1.call-done, bf16[]{:T(256)} %constant.106.clone.1), kind=kCustom, calls=%fused_computation.24 | custom fusion | bytes 1049344 | tf_op jit(solution)/shard_map/scatter | solution.py:30
  190.5 0.1 slice.16
  190.6 0.2 convert.3
  190.8 2.2 fusion.2
  193.0 2.1 convolution_bitcast_fusion.1
  195.2 4.1 %fusion.1 = f32[64,64,128]{2,0,1:T(8,128)S(1)} fusion(f32[64,64,128]{2,1,0:T(8,128)S(1)} %convolution_bitcast_fusion.1, f32[128]{0:T(128)S(1)} %fusion.47, f32[64,64]{0,1:T(8,128)S(1)} %broadcast_add_fusion), kind=kOutput, calls=%fused_computation.6 | convolution fusion | flops 408481792 | bytes 4211200 | tf_op jit(solution)/shard_map/bxdc,xe->bedc/dot_general | solution.py:60
  199.3 3.5 %fusion.7 = f32[64,64,128]{2,1,0:T(8,128)S(1)} fusion(f32[64,64,128]{2,0,1:T(8,128)S(1)} %fusion.1), kind=kOutput, calls=%fused_computation.14 | convolution fusion | flops 805552128 | bytes 4194304 | tf_op jit(solution)/shard_map/bxyz,zc->bxyc/dot_general | solution.py:58
  202.8 2.4 %convolution_bitcast_fusion = f32[64,64,128]{2,1,0:T(8,128)S(1)} fusion(f32[64,64,128]{2,1,0:T(8,128)S(1)} %fusion.7), kind=kOutput, calls=%fused_computation.18 | convolution fusion | flops 402714624 | bytes 4194304 | tf_op jit(solution)/shard_map/bxyc,yd->bxdc/dot_general | solution.py:59
  205.2 4.3 %fusion.15 = bf16[1,64,64,128]{3,1,2,0:T(8,128)(2,1)S(1)} fusion(f32[64,64,128]{2,1,0:T(8,128)S(1)} %convolution_bitcast_fusion, f32[64,64,128]{2,1,0:T(8,128)S(1)} %convert.3), kind=kOutput, calls=%fused_computation.20 | convolution fusion | flops 404811776 | bytes 5242880 | tf_op jit(solution)/shard_map/bxdc,xe->bedc/dot_general | solution.py:60
  209.5 1.6 copy.14
  (4 shorter events, 0.0 us)
Async XLA Ops:
  6.5 113.7 %copy-start = (s32[4096]{0:T(1024)S(1)}, s32[4096]{0:T(1024)}, u32[]{:S(2)}) copy-start(s32[4096]{0:T(1024)} %param.5) | copy-start | bytes 49156
  6.5 106.3 %all-gather.3.cloned.1.call-start = ((), (), s32[]{:S(2)}) async-start(), calls=%async_computation.1 | async-start | bytes 13369344 | tf_op jit(solution)/shard_map/all_gather | solution.py:15
  9.3 4.3 %copy-start.2 = (s32[2]{0:T(128)S(1)}, s32[2]{0:T(128)}, u32[]{:S(2)}) copy-start(s32[2]{0:T(128)} %param.6) | copy-start | bytes 28
  9.3 146.7 %all-to-all-start = ((bf16[2,3072,128]{2,1,0:T(8,128)(2,1)}), bf16[2,3072,128]{2,1,0:T(8,128)(2,1)S(1)}, u32[]{:S(2)}, u32[]{:S(2)}) async-start(bf16[2,3072,128]{2,1,0:T(8,128)(2,1)} %param.4), calls=%async_computation | async-start | bytes 3145728 | tf_op jit(solution)/shard_map/all_to_all | solution.py:67
  13.6 160.2 %all-gather.5.cloned.1.call-start = ((), (), s32[]{:S(2)}) async-start(), calls=%async_computation.2 | async-start | bytes 2359296 | tf_op jit(solution)/shard_map/all_gather | solution.py:78
  156.1 1.2 copy-start.1
Sparse Core Ops, SparseCore 0:
  9.6 103.1 all-gather.2
  120.4 25.4 all-gather.4
